TPU v7x, 32 devices: a whole 2x2x4 slice. The times are simulated.
32 devices in a mesh: grp: 4 (over z), ep: 4 (over y, x), tp: 2 (over core).
Axes of the slice: x: 2, y: 2, z: 4, core: 2. Of those that a mesh axis runs over, the one named last changes fastest.
Arguments:
- tokens: bfloat16 [128, 7168], P('ep', 'tp'), may hold values from -6 to 6
- gates: float32 [128, 8], P('ep'), may hold values from 0.05 to 1
- expert_ids: int32 [128, 8], P('ep'), may hold values from 0 to 31, all different within a row; in each aligned block of 16 rows (0 to 15, 16 to 31, ...) at most 8 rows name the same one
- gate_weight: bfloat16 [32, 7168, 2048], P('ep', None, ('grp', 'tp')), may hold values from -0.0625 to 0.0625
- up_weight: bfloat16 [32, 7168, 2048], P('ep', None, ('grp', 'tp')), may hold values from -0.0625 to 0.0625
- down_weight: bfloat16 [32, 2048, 7168], P('ep', ('grp', 'tp')), may hold values from -0.125 to 0.125
Outputs:
- mixed_out: bfloat16 [128, 7168], P('ep', ('grp', 'tp'))
Inputs may be any that keep to these rules, and one draw needn't show every extreme that they name: `expert_ids`: within each aligned block of 16 rows, the 8 experts of a row differ, and no expert is named by more than 8 rows; some expert is named by exactly 8 rows in some blocks.
All inputs are finite; a program needn't handle non-finite values.
Results may differ from a plain program's by a relative error of at most 0.013.
Values may be sent and summed in bfloat16 or wider, within the bound.
A program may use at most 192 MiB of HBM per device.

v0:
```python
import jax
import jax.numpy as jnp
from jax import lax
from jax.sharding import PartitionSpec as P

TOP = 8
EXPERTS = 32
MB = 2
CAP = 8


def local(tokens, gates, expert_ids, gate_weight, up_weight, down_weight):
    experts_here = gate_weight.shape[0]
    per_micro = tokens.shape[0] // MB
    half_width = tokens.shape[1]
    full_width = down_weight.shape[2]
    sources = lax.axis_size("ep")
    slots = EXPERTS * CAP
    share = full_width // (lax.axis_size("grp") * lax.axis_size("tp"))
    results = []
    for micro in range(MB):
        rows_in = tokens[micro * per_micro : (micro + 1) * per_micro]
        chosen = expert_ids[micro * per_micro : (micro + 1) * per_micro]
        weights = gates[micro * per_micro : (micro + 1) * per_micro]
        flat = chosen.reshape(-1)
        onehot = (flat[:, None] == lax.iota(jnp.int32, EXPERTS)[None, :]).astype(jnp.int32)
        before = jnp.cumsum(onehot, axis=0) - onehot
        slot = jnp.sum(before * onehot, axis=1)
        target = (flat * CAP + slot).reshape(per_micro, TOP)
        match = (target[None, :, :] == lax.iota(jnp.int32, slots)[:, None, None]).astype(
            jnp.float32
        )
        placing = jnp.sum(match, axis=2).astype(jnp.bfloat16)
        mixing = jnp.transpose(jnp.sum(match * weights[None, :, :], axis=2))
        sent = jnp.dot(placing, rows_in, preferred_element_type=jnp.float32).astype(jnp.bfloat16)
        sent = sent.reshape(EXPERTS, CAP, half_width)
        arrived = lax.all_to_all(sent, "ep", split_axis=0, concat_axis=0, tiled=True)
        piece = lax.all_gather(arrived, "tp", axis=2, tiled=True)
        count = piece.shape[2]
        blocked = piece.reshape(sources, experts_here, CAP, count)
        gate_part = jnp.einsum(
            "secd,edh->sech", blocked, gate_weight, preferred_element_type=jnp.float32
        )
        up_part = jnp.einsum(
            "secd,edh->sech", blocked, up_weight, preferred_element_type=jnp.float32
        )
        hidden = (jax.nn.silu(gate_part) * up_part).astype(jnp.bfloat16)
        term = jnp.einsum("sech,ehd->dsec", hidden, down_weight, preferred_element_type=jnp.float32)
        summed = lax.psum_scatter(
            term.reshape(share * lax.axis_size(("grp", "tp")), sources * experts_here * CAP),
            ("grp", "tp"),
            scatter_dimension=0,
            tiled=True,
        )
        expert_out = summed.astype(jnp.bfloat16)
        returned = lax.all_to_all(expert_out, "ep", split_axis=1, concat_axis=1, tiled=True)
        mixed = lax.dot_general(
            mixing,
            returned.astype(jnp.float32),
            (((1,), (1,)), ((), ())),
            precision=lax.Precision.HIGHEST,
        )
        results.append(mixed.astype(jnp.bfloat16))
    return jnp.concatenate(results, axis=0)


def solution(mesh):
    placed = (
        P("ep", "tp"),
        P("ep", None),
        P("ep", None),
        P("ep", None, ("grp", "tp")),
        P("ep", None, ("grp", "tp")),
        P("ep", ("grp", "tp"), None),
    )
    return jax.shard_map(
        local, mesh=mesh, in_specs=placed, out_specs=P("ep", ("grp", "tp")), check_vma=False
    )
```

profile of v0, /device:TPU:0, one launch (start us, length us, event | category | flops | bytes accessed | tf_op | source)
XLA Modules:
  0.0 296.6 jit_solution(6247645998715472486)
XLA Ops:
  6.5 0.8 fusion.93
  7.5 0.1 fusion.86
  7.6 0.2 reduce_window_sum.18
  7.8 0.2 select_reduce_fusion.2
  8.1 0.8 fusion.92
  9.0 0.1 convert_reduce_fusion
  9.2 1.6 fusion.19
  10.7 27.7 %all_to_all.34 = bf16[32,8,3584]{2,1,0:T(8,128)(2,1)} all-to-all(bf16[32,8,3584]{2,1,0:T(8,128)(2,1)S(1)} %fusion.19), channel_id=1, replica_groups=mesh['grp'=4,'ep'=4,'tp'=2] {'ep'}, dimensions={0} | all-to-all | bytes 3670016 | tf_op jit(solution)/shard_map/all_to_all | solution.py:37
  38.5 0.1 eq.56
  38.6 0.1 fusion.87
  38.7 0.2 reduce_window_sum.17
  38.9 0.2 select_reduce_fusion.3
  39.2 0.2 convert_reduce_fusion.1
  39.4 0.7 fusion.18
  40.1 24.6 %all_to_all.35 = bf16[32,8,3584]{2,1,0:T(8,128)(2,1)} all-to-all(bf16[32,8,3584]{2,1,0:T(8,128)(2,1)S(1)} %fusion.18), channel_id=1, replica_groups=mesh['grp'=4,'ep'=4,'tp'=2] {'ep'}, dimensions={0} | all-to-all | bytes 3670016 | tf_op jit(solution)/shard_map/all_to_all | solution.py:37
  64.7 17.1 %fusion.29 = f32[4,8,8,256]{3,2,0,1:T(8,128)S(1)} fusion(bf16[8,7168,256]{2,1,0:T(8,128)(2,1)} %param.9, bf16[4,8,8,7168]{3,2,1,0:T(8,128)(2,1)} %bitcast.89), kind=kOutput, calls=%fused_computation.23 | convolution fusion | flops 939524096 | bytes 33292288 | tf_op jit(solution)/shard_map/secd,edh->sech/dot_general | solution.py:41
  81.8 28.7 %fusion.15 = f32[7168,4,8,8]{0,3,1,2:T(8,128)} fusion(bf16[8,256,7168]{2,1,0:T(8,128)(2,1)} %param.11, bf16[8,7168,256]{2,1,0:T(8,128)(2,1)} %param.10, bf16[4,8,8,7168]{3,2,1,0:T(8,128)(2,1)} %bitcast.90, f32[4,8,8,256]{3,2,0,1:T(8,128)S(1)} %fusion.29), kind=kOutput, calls=%fused_computation.13 | convolution fusion | flops 1879441408 | bytes 69992448 | tf_op jit(solution)/shard_map/sech,ehd->dsec/dot_general | solution.py:48
  110.5 6.8 %copy.28 = f32[7168,4,8,8]{0,3,2,1:T(8,128)} copy(f32[7168,4,8,8]{0,3,1,2:T(8,128)} %fusion.15) | data formatting | bytes 14680064 | tf_op jit(solution)/shard_map/sech,ehd->dsec/transpose | solution.py:48
  117.4 0.2 reduce-scatter.3.cloned.1.call-start
  117.7 15.9 %fusion.24 = f32[4,8,8,256]{3,2,0,1:T(8,128)S(1)} fusion(bf16[8,7168,256]{2,1,0:T(8,128)(2,1)} %param.9, bf16[4,8,8,7168]{3,2,1,0:T(8,128)(2,1)} %bitcast.91), kind=kOutput, calls=%fused_computation.22 | convolution fusion | flops 939524096 | bytes 33292288 | tf_op jit(solution)/shard_map/secd,edh->sech/dot_general | solution.py:41
  133.6 29.2 %fusion.12 = f32[7168,4,8,8]{0,3,1,2:T(8,128)} fusion(bf16[8,256,7168]{2,1,0:T(8,128)(2,1)} %param.11, bf16[8,7168,256]{2,1,0:T(8,128)(2,1)} %param.10, bf16[4,8,8,7168]{3,2,1,0:T(8,128)(2,1)} %bitcast.92, f32[4,8,8,256]{3,2,0,1:T(8,128)S(1)} %fusion.24), kind=kOutput, calls=%fused_computation.12 | convolution fusion | flops 1879441408 | bytes 69992448 | tf_op jit(solution)/shard_map/sech,ehd->dsec/dot_general | solution.py:48
  162.8 7.0 %copy.23 = f32[7168,4,8,8]{0,3,2,1:T(8,128)} copy(f32[7168,4,8,8]{0,3,1,2:T(8,128)} %fusion.12) | data formatting | bytes 14680064 | tf_op jit(solution)/shard_map/sech,ehd->dsec/transpose | solution.py:48
  169.8 27.1 %reduce-scatter.5.cloned.1.call-done = f32[896,256]{0,1:T(8,128)} async-done(((f32[7168,256]{0,1:T(8,128)}), f32[896,256]{0,1:T(8,128)}) %reduce-scatter.5.cloned.1.call-update) | async-done | bytes 917520 | tf_op jit(solution)/shard_map/reduce_scatter | solution.py:49
  196.9 2.0 convert_element_type.56
  198.9 3.6 %all-to-all-start.3 = ((bf16[896,4,64]{0,2,1:T(8,128)(2,1)}), bf16[896,4,64]{0,2,1:T(8,128)(2,1)S(1)}, u32[]{:S(2)}, u32[]{:S(2)}) async-start(bf16[896,4,64]{0,2,1:T(8,128)(2,1)} %bitcast.23), calls=%async_computation.5 | async-start | bytes 917504 | tf_op jit(solution)/shard_map/all_to_all | solution.py:56
  202.6 74.6 %reduce-scatter.3.cloned.1.call-done = f32[896,256]{0,1:T(8,128)} async-done(((f32[7168,256]{0,1:T(8,128)}), f32[896,256]{0,1:T(8,128)}) %reduce-scatter.3.cloned.1.call-update) | async-done | bytes 917520 | tf_op jit(solution)/shard_map/reduce_scatter | solution.py:49
  277.2 2.0 convert_element_type.49
  279.2 3.6 %all-to-all-start.1 = ((bf16[896,4,64]{0,2,1:T(8,128)(2,1)}), bf16[896,4,64]{0,2,1:T(8,128)(2,1)S(1)}, u32[]{:S(2)}, u32[]{:S(2)}) async-start(bf16[896,4,64]{0,2,1:T(8,128)(2,1)} %bitcast.12), calls=%async_computation.2 | async-start | bytes 917504 | tf_op jit(solution)/shard_map/all_to_all | solution.py:56
  282.9 0.3 convolution_convert_fusion.2
  283.1 5.9 %all-to-all-done.1 = bf16[896,4,64]{0,2,1:T(8,128)(2,1)S(1)} async-done(((bf16[896,4,64]{0,2,1:T(8,128)(2,1)}), bf16[896,4,64]{0,2,1:T(8,128)(2,1)S(1)}, u32[]{:S(2)}, u32[]{:S(2)}) %all-to-all-start.1) | async-done | bytes 458784 | tf_op jit(solution)/shard_map/all_to_all | solution.py:56
  289.1 0.3 convolution_convert_fusion.3
  289.4 0.6 pad_maximum_fusion
  (21 shorter events, 0.8 us)
Async XLA Ops:
  6.5 32.9 %copy-start = (bf16[32,3584]{1,0:T(8,128)(2,1)S(1)}, bf16[32,3584]{1,0:T(8,128)(2,1)}, u32[]{:S(2)}) copy-start(bf16[32,3584]{1,0:T(8,128)(2,1)} %param.6) | copy-start | bytes 688132
  6.5 58.2 %all-gather.5.cloned.1.call-start = ((), (), s32[]{:S(2)}) async-start(), calls=%async_computation.8 | async-start | bytes 5505024 | tf_op jit(solution)/shard_map/all_gather | solution.py:38
  38.4 79.3 %all-gather.3.cloned.1.call-start = ((), (), s32[]{:S(2)}) async-start(), calls=%async_computation.6 | async-start | bytes 5505024 | tf_op jit(solution)/shard_map/all_gather | solution.py:38
  64.7 132.2 %reduce-scatter.5.cloned.1.call-start = ((), (), s32[]{:S(2)}) async-start(), calls=%async_computation.9 | async-start | bytes 8257536 | tf_op jit(solution)/shard_map/reduce_scatter | solution.py:49
  117.4 159.8 %reduce-scatter.3.cloned.1.call-start = ((), (), s32[]{:S(2)}) async-start(), calls=%async_computation.7 | async-start | bytes 8257536 | tf_op jit(solution)/shard_map/reduce_scatter | solution.py:49
  198.9 80.3 %all-to-all-start.3 = ((bf16[896,4,64]{0,2,1:T(8,128)(2,1)}), bf16[896,4,64]{0,2,1:T(8,128)(2,1)S(1)}, u32[]{:S(2)}, u32[]{:S(2)}) async-start(bf16[896,4,64]{0,2,1:T(8,128)(2,1)} %bitcast.23), calls=%async_computation.5 | async-start | bytes 917504 | tf_op jit(solution)/shard_map/all_to_all | solution.py:56
  279.2 9.9 %all-to-all-start.1 = ((bf16[896,4,64]{0,2,1:T(8,128)(2,1)}), bf16[896,4,64]{0,2,1:T(8,128)(2,1)S(1)}, u32[]{:S(2)}, u32[]{:S(2)}) async-start(bf16[896,4,64]{0,2,1:T(8,128)(2,1)} %bitcast.12), calls=%async_computation.2 | async-start | bytes 917504 | tf_op jit(solution)/shard_map/all_to_all | solution.py:56
Sparse Core Ops, SparseCore 0:
  38.5 12.6 all-gather.4
  64.8 12.6 all-gather.2
  117.5 79.3 reduce-scatter.4
  199.1 78.0 reduce-scatter.2
where the time goes:
time: 297 us
  waiting for transfers between devices  108 us (36%)
  matrix products  93.7 us (32%)
  blocking collectives  52.2 us (18%)
  local copies, waits for them, and re-layouts  16.1 us (5%)
  between operations  13.2 us (4%)
  starting transfers between devices  7.6 us (3%)
  other arithmetic  5.85 us (2%)
    reduce_scatter x2, waiting for transfers between devices, local(): lax.psum_scatter(term.reshape(share * lax.axis_size(('grp', 'tp')), sourc...  102 us
    dot_general x2, matrix products, local(): jnp.einsum('sech,ehd->dsec', hidden, down_weight, preferred_element_type=...  57.9 us
    all_to_all x2, blocking collectives, local(): lax.all_to_all(sent, 'ep', split_axis=0, concat_axis=0, tiled=True)  52.2 us
    dot_general x2, matrix products, local(): jnp.einsum('secd,edh->sech', blocked, gate_weight, preferred_element_type...  33 us
    transpose x2, local copies, waits for them, and re-layouts, local(): jnp.einsum('sech,ehd->dsec', hidden, down_weight, preferred_element_type=...  13.8 us
    all_to_all x2, starting transfers between devices, local(): lax.all_to_all(expert_out, 'ep', split_axis=1, concat_axis=1, tiled=True)  7.3 us
  transfers between devices with their start and end apart: 6, of which 3 were waited for; matrix products, arithmetic and copies ran while one was open for 37% of the time, Pallas kernels for 0%

commit v1 on v0

v1 whole, which is shorter than its diff:
```python
import functools

import jax
import jax.numpy as jnp
from jax import lax
from jax.experimental import pallas as pl
from jax.experimental.pallas import tpu as pltpu
from jax.sharding import PartitionSpec as P

MESH = pl.DeviceIdType.MESH
EXPERT_SLOTS = 5
DOWN_SLOTS = 4
ROW_BLOCK = 256


def kernel(
    ep, grp, tp,
    tok, gates, ids, wg, wu, wd, out,
    x, gall, iall, wgb, wub, wdb, hid, own, tsend, trecv, psend, xyrecv, zsend, zrecv,
    w_sem, d_sem, loc_sem, ag_s, ag_r, gt_s, gt_r, id_s, id_r, f_s, f_r,
    t_s, t_r, xy_s, xy_r, z_s, z_r,
):
    me_ep, me_grp, me_tp = lax.axis_index("ep"), lax.axis_index("grp"), lax.axis_index("tp")
    mate = 1 - me_tp
    experts, width, units = wg.shape
    rows, half = tok.shape
    share = out.shape[1]
    total = rows * ep
    slots = wgb.shape[0]
    down_slots = wdb.shape[0]
    chunks = grp * tp

    def at_rows(index):
        return pl.ds(pl.multiple_of(index * rows, rows), rows)

    def expert_copies(e):
        s = lax.rem(e, slots)
        return (
            pltpu.make_async_copy(wg.at[e], wgb.at[s], w_sem.at[s, 0]),
            pltpu.make_async_copy(wu.at[e], wub.at[s], w_sem.at[s, 1]),
        )

    def group_of(i):
        return lax.rem(me_grp + 1 + i, grp)

    def down_copy(c):
        s = lax.rem(c, down_slots)
        i, second = c // 2, lax.rem(c, 2)
        column = group_of(i) * 2 + lax.rem(mate + second, 2)
        return pltpu.make_async_copy(
            wd.at[:, pl.ds(pl.multiple_of(column * share, 128), share)], wdb.at[s], d_sem.at[s]
        )

    def start_expert(e):
        for copy in expert_copies(e):
            copy.start()

    for e in range(slots):
        start_expert(jnp.int32(e))
    own_rows = pltpu.make_async_copy(tok, x.at[me_tp, at_rows(me_ep)], loc_sem.at[0])
    own_rows.start()

    barrier = pltpu.get_barrier_semaphore()

    @pl.loop(1, ep)
    def _(d):
        pl.semaphore_signal(
            barrier, inc=1, device_id={"ep": lax.rem(me_ep + d, ep)}, device_id_type=MESH
        )

    @pl.loop(1, grp)
    def _(d):
        pl.semaphore_signal(
            barrier, inc=1, device_id={"grp": lax.rem(me_grp + d, grp)}, device_id_type=MESH
        )

    pl.semaphore_signal(barrier, inc=1, device_id={"tp": mate}, device_id_type=MESH)
    pl.semaphore_wait(barrier, ep + grp - 1)

    def gather_copies(d):
        to = {"ep": lax.rem(me_ep + d, ep)}
        mine = at_rows(me_ep)
        return (
            pltpu.make_async_remote_copy(
                tok, x.at[me_tp, mine], ag_s.at[d], ag_r.at[d], to, MESH
            ),
            pltpu.make_async_remote_copy(
                gates, gall.at[me_ep], gt_s.at[d], gt_r.at[d], to, MESH
            ),
            pltpu.make_async_remote_copy(
                ids, iall.at[me_ep], id_s.at[d], id_r.at[d], to, MESH
            ),
        )

    def pass_on(d):
        where = x.at[me_tp, at_rows(lax.rem(me_ep - d + ep, ep))]
        return pltpu.make_async_remote_copy(
            where, where, f_s.at[d], f_r.at[d], {"tp": mate}, MESH
        )

    def pass_own():
        return pltpu.make_async_remote_copy(
            tok, x.at[me_tp, at_rows(me_ep)], f_s.at[0], f_r.at[0], {"tp": mate}, MESH
        )

    @pl.loop(1, ep)
    def _(d):
        for copy in gather_copies(d):
            copy.start()

    pass_own().start()
    for c in range(down_slots):
        down_copy(jnp.int32(c)).start()
    gall[me_ep] = gates[...]
    iall[me_ep] = ids[...]

    @pl.loop(1, ep)
    def _(d):
        gather_copies(d)[0].wait_recv()
        pass_on(d).start()

    own_rows.wait()
    pass_own().wait_recv()

    @pl.loop(1, ep)
    def _(d):
        pass_on(d).wait_recv()
        for copy in gather_copies(d)[1:]:
            copy.wait_recv()

    block = min(total, ROW_BLOCK)

    def by_rows(body):
        if block == total:
            body(0)
        else:
            pl.loop(0, total // block)(lambda b: body(pl.multiple_of(b * block, block)))

    per_block = block // rows

    @pl.loop(0, experts)
    def _(e):
        s = lax.rem(e, slots)
        for copy in expert_copies(e):
            copy.wait()
        number = me_ep * experts + e

        def body(start):
            def project(w):
                parts = [
                    jnp.dot(
                        x[t, pl.ds(start, block), :],
                        w[s, t * half : (t + 1) * half, :],
                        preferred_element_type=jnp.float32,
                    )
                    for t in range(tp)
                ]
                return functools.reduce(jnp.add, parts)

            gate, up = project(wgb), project(wub)
            first = start // rows
            chosen = iall[pl.ds(first, per_block)].reshape(block, ids.shape[1])
            weights = gall[pl.ds(first, per_block)].reshape(block, ids.shape[1])
            scale = jnp.sum(
                jnp.where(chosen == number, weights, 0.0), axis=1, keepdims=True
            )
            value = gate / (1.0 + jnp.exp(-gate)) * up * scale
            hid[pl.ds(start, block), pl.ds(pl.multiple_of(e * units, units), units)] = (
                value.astype(hid.dtype)
            )

        by_rows(body)

        @pl.when(e + slots < experts)
        def _():
            start_expert(e + slots)

    def project_down(c, target):
        s = lax.rem(c, down_slots)
        down_copy(c).wait()

        def body(start):
            where = pl.ds(start, block)
            target[where, :] = jnp.dot(
                hid[where, :], wdb[s], preferred_element_type=jnp.float32
            ).astype(target.dtype)

        by_rows(body)

        @pl.when(c + down_slots < chunks)
        def _():
            down_copy(c + down_slots).start()

    def to_mate(i):
        return pltpu.make_async_remote_copy(
            tsend.at[i], trecv.at[i], t_s.at[i], t_r.at[i], {"tp": mate}, MESH
        )

    def to_source(i, d):
        peer = lax.rem(me_ep + d, ep)
        return pltpu.make_async_remote_copy(
            psend.at[i, at_rows(peer)], xyrecv.at[i, d], xy_s.at[i, d], xy_r.at[i, d],
            {"ep": peer}, MESH,
        )

    def to_group(i):
        return pltpu.make_async_remote_copy(
            zsend.at[i], zrecv.at[i], z_s.at[i], z_r.at[i], {"grp": group_of(i)}, MESH
        )

    def add_mate(i):
        to_mate(i).wait_recv()

        def body(start):
            where = pl.ds(start, block)
            psend[i, where, :] = (own[where, :] + trecv[i, where, :].astype(jnp.float32)).astype(
                psend.dtype
            )

        by_rows(body)
        pl.loop(1, ep)(lambda d: to_source(i, d).start())

    def add_sources(i):
        pl.loop(1, ep)(lambda d: to_source(i, d).wait_recv())
        mine = psend[i, at_rows(me_ep), :].astype(jnp.float32)
        return lax.fori_loop(
            1, ep, lambda d, acc: acc + xyrecv[i, d].astype(jnp.float32), mine
        )

    def add_and_send(i):
        zsend[i] = add_sources(i).astype(zsend.dtype)
        to_group(i).start()

    @pl.loop(0, grp)
    def _(i):
        project_down(2 * i, tsend.at[i])
        to_mate(i).start()

        @pl.when(i > 0)
        def _():
            add_mate(i - 1)

        project_down(2 * i + 1, own)

        @pl.when(i > 0)
        def _():
            add_and_send(i - 1)

    add_mate(grp - 1)
    result = add_sources(grp - 1)
    for i in range(grp - 1):
        to_group(i).wait_recv()
        result = result + zrecv[i].astype(jnp.float32)
    out[...] = result.astype(out.dtype)

    pass_own().wait_send()

    @pl.loop(1, ep)
    def _(d):
        for copy in gather_copies(d):
            copy.wait_send()
        pass_on(d).wait_send()

    @pl.loop(0, grp)
    def _(i):
        to_mate(i).wait_send()
        pl.loop(1, ep)(lambda d: to_source(i, d).wait_send())

    pl.loop(0, grp - 1)(lambda i: to_group(i).wait_send())


def local(tokens, gates, expert_ids, gate_weight, up_weight, down_weight):
    ep, grp, tp = lax.axis_size("ep"), lax.axis_size("grp"), lax.axis_size("tp")
    rows, half = tokens.shape
    experts, width, units = gate_weight.shape
    share = width // (grp * tp)
    total = rows * ep
    top = gates.shape[1]
    slots = min(EXPERT_SLOTS, experts)
    bf16, f32 = jnp.bfloat16, jnp.float32
    down = down_weight.reshape(experts * units, width)
    down_slots = min(DOWN_SLOTS, grp * tp)
    dma = pltpu.SemaphoreType.DMA
    vmem = pl.BlockSpec(memory_space=pltpu.VMEM)
    hbm = pl.BlockSpec(memory_space=pl.ANY)
    return pl.pallas_call(
        functools.partial(kernel, ep, grp, tp),
        out_shape=jax.ShapeDtypeStruct((rows, share), bf16),
        in_specs=[hbm, vmem, vmem, hbm, hbm, hbm],
        out_specs=vmem,
        scratch_shapes=[
            pltpu.VMEM((tp, total, half), bf16),
            pltpu.VMEM((ep, rows, top), f32),
            pltpu.VMEM((ep, rows, top), jnp.int32),
            pltpu.VMEM((slots, width, units), bf16),
            pltpu.VMEM((slots, width, units), bf16),
            pltpu.VMEM((down_slots, experts * units, share), bf16),
            pltpu.VMEM((total, experts * units), bf16),
            pltpu.VMEM((total, share), f32),
            pltpu.VMEM((grp, total, share), bf16),
            pltpu.VMEM((grp, total, share), bf16),
            pltpu.VMEM((grp, total, share), bf16),
            pltpu.VMEM((grp, ep, rows, share), bf16),
            pltpu.VMEM((grp, rows, share), bf16),
            pltpu.VMEM((grp, rows, share), bf16),
            dma((slots, 2)), dma((down_slots,)), dma((1,)),
            dma((ep,)), dma((ep,)), dma((ep,)), dma((ep,)), dma((ep,)), dma((ep,)),
            dma((ep,)), dma((ep,)),
            dma((grp,)), dma((grp,)), dma((grp, ep)), dma((grp, ep)), dma((grp,)), dma((grp,)),
        ],
        compiler_params=pltpu.CompilerParams(
            collective_id=0, has_side_effects=True, vmem_limit_bytes=66_000_000
        ),
    )(tokens, gates, expert_ids, gate_weight, up_weight, down)


def solution(mesh):
    placed = (
        P("ep", "tp"),
        P("ep", None),
        P("ep", None),
        P("ep", None, ("grp", "tp")),
        P("ep", None, ("grp", "tp")),
        P("ep", ("grp", "tp"), None),
    )
    return jax.shard_map(
        local, mesh=mesh, in_specs=placed, out_specs=P("ep", ("grp", "tp")), check_vma=False
    )
```

time: 297 us -> 57.6 us (0.19)
  waiting for transfers between devices: 108 us -> 0 us
  matrix products: 93.7 us -> 0 us
  Pallas kernels: 0 us -> 53 us
  blocking collectives: 52.2 us -> 0 us
  between operations: 13.2 us -> 0.01 us
  local copies, waits for them, and re-layouts: 16.1 us -> 4.17 us
  starting transfers between devices: 7.6 us -> 0 us
  other arithmetic: 5.85 us -> 0 us
    reduce_scatter x2 -> x0, waiting for transfers between devices: 102 us -> none  [local(): lax.psum_scatter(term.reshape(share * lax.axis_size(('grp', 'tp')), sourc...]
    dot_general x8 -> x0, matrix products: 93.7 us -> none  [the longest x2 57.9 us: local(): jnp.einsum('sech,ehd->dsec', hidden, down_weight, preferred_element_type=...]
    pallas_call x0 -> x1, Pallas kernels: none -> 53 us  [local(): pl.pallas_call(functools.partial(kernel, ep, grp, tp), out_shape=jax.Shap...]
    all_to_all x2 -> x0, blocking collectives: 52.2 us -> none  [local(): lax.all_to_all(sent, 'ep', split_axis=0, concat_axis=0, tiled=True)]
    transpose x2 -> x0, local copies, waits for them, and re-layouts: 13.8 us -> none  [local(): jnp.einsum('sech,ehd->dsec', hidden, down_weight, preferred_element_type=...]
    all_to_all x2 -> x0, starting transfers between devices: 7.3 us -> none  [local(): lax.all_to_all(expert_out, 'ep', split_axis=1, concat_axis=1, tiled=True)]
    all_to_all x2 -> x0, waiting for transfers between devices: 5.94 us -> none  [local(): lax.all_to_all(expert_out, 'ep', split_axis=1, concat_axis=1, tiled=True)]
    convert_element_type x4 -> x0, other arithmetic: 4.18 us -> none  [the longest x2 4.01 us: local(): expert_out = summed.astype(jnp.bfloat16)]
  transfers between devices with their start and end apart: 6 -> 0, of which waited for: 3 -> 0; matrix products, arithmetic and copies ran while one was open for 37% -> 0% of each run, Pallas kernels for 0% -> 0%
where the time goes in v1:
time: 57.6 us; the launch traced here: 57.2 us
  Pallas kernels  53 us (92%)
  local copies, waits for them, and re-layouts  4.17 us (7%)
    pallas_call x1, Pallas kernels, local(): pl.pallas_call(functools.partial(kernel, ep, grp, tp), out_shape=jax.Shap...  53 us
    unnamed x3, local copies, waits for them, and re-layouts  4.17 us

profile of v1, /device:TPU:0, one launch (start us, length us, event | category | flops | bytes accessed | tf_op | source)
XLA Modules:
  0.0 57.2 jit_solution(5437684636354695358)
XLA Ops:
  0.0 1.4 %copy.7.gates = f32[32,8]{1,0:T(8,128)} copy(f32[32,8]{0,1:T(8,128)} %param.7) | data formatting | bytes 2048 | tf_op args[1]
  1.4 1.4 %copy.8.ids = s32[32,8]{1,0:T(8,128)} copy(s32[32,8]{0,1:T(8,128)} %param.8) | data formatting | bytes 2048 | tf_op args[2]
  2.7 53.0 %shard_map.64 = bf16[32,896]{1,0:T(8,128)(2,1)} custom-call(bf16[32,3584]{1,0:T(8,128)(2,1)} %tok.1, f32[32,8]{1,0:T(8,128)} %copy.7.gates, s32[32,8]{1,0:T(8,128)} %copy.8.ids, bf16[8,7168,256]{2,1,0:T(8,128)(2,1)} %wg.1, bf16[8,7168,256]{2,1,0:T(8,128)(2,1)} %wu.1, bf16[2048,7168]{1,0:T(8,128)(2,1)} %bitcast.1), custom_call_target="tpu_custom_call" | custom-call | tf_op jit(solution)/shard_map/pallas_call | solution.py:286
  55.8 1.4 %copy.10 = bf16[32,896]{1,0:T(8,128)(2,1)} copy(bf16[32,896]{1,0:T(8,128)(2,1)} %shard_map.64) | data formatting | bytes 114688

commit v2 on v1

--- a/solution.py
+++ b/solution.py
@@ -11,6 +11,7 @@
 EXPERT_SLOTS = 5
 DOWN_SLOTS = 4
 ROW_BLOCK = 256
+PIECES = 2
 
 
 def kernel(
@@ -77,13 +78,18 @@
     pl.semaphore_signal(barrier, inc=1, device_id={"tp": mate}, device_id_type=MESH)
     pl.semaphore_wait(barrier, ep + grp - 1)
 
-    def gather_copies(d):
+    piece = half // PIECES
+
+    def gather_piece(d, p):
+        cols = pl.ds(p * piece, piece)
+        return pltpu.make_async_remote_copy(
+            tok.at[:, cols], x.at[me_tp, at_rows(me_ep), cols], ag_s.at[d, p], ag_r.at[d, p],
+            {"ep": lax.rem(me_ep + d, ep)}, MESH,
+        )
+
+    def gather_routes(d):
         to = {"ep": lax.rem(me_ep + d, ep)}
-        mine = at_rows(me_ep)
         return (
-            pltpu.make_async_remote_copy(
-                tok, x.at[me_tp, mine], ag_s.at[d], ag_r.at[d], to, MESH
-            ),
             pltpu.make_async_remote_copy(
                 gates, gall.at[me_ep], gt_s.at[d], gt_r.at[d], to, MESH
             ),
@@ -92,20 +98,23 @@
             ),
         )
 
-    def pass_on(d):
-        where = x.at[me_tp, at_rows(lax.rem(me_ep - d + ep, ep))]
-        return pltpu.make_async_remote_copy(
-            where, where, f_s.at[d], f_r.at[d], {"tp": mate}, MESH
+    def pass_on(d, p):
+        where = x.at[me_tp, at_rows(lax.rem(me_ep - d + ep, ep)), pl.ds(p * piece, piece)]
+        return pltpu.make_async_remote_copy(
+            where, where, f_s.at[d, p], f_r.at[d, p], {"tp": mate}, MESH
         )
 
     def pass_own():
         return pltpu.make_async_remote_copy(
-            tok, x.at[me_tp, at_rows(me_ep)], f_s.at[0], f_r.at[0], {"tp": mate}, MESH
-        )
+            tok, x.at[me_tp, at_rows(me_ep)], f_s.at[0, 0], f_r.at[0, 0], {"tp": mate}, MESH
+        )
+
+    for p in range(PIECES):
+        pl.loop(1, ep)(lambda d: gather_piece(d, p).start())
 
     @pl.loop(1, ep)
     def _(d):
-        for copy in gather_copies(d):
+        for copy in gather_routes(d):
             copy.start()
 
     pass_own().start()
@@ -114,18 +123,21 @@
     gall[me_ep] = gates[...]
     iall[me_ep] = ids[...]
 
-    @pl.loop(1, ep)
-    def _(d):
-        gather_copies(d)[0].wait_recv()
-        pass_on(d).start()
+    for p in range(PIECES):
+
+        @pl.loop(1, ep)
+        def _(d):
+            gather_piece(d, p).wait_recv()
+            pass_on(d, p).start()
 
     own_rows.wait()
     pass_own().wait_recv()
 
     @pl.loop(1, ep)
     def _(d):
-        pass_on(d).wait_recv()
-        for copy in gather_copies(d)[1:]:
+        for p in range(PIECES):
+            pass_on(d, p).wait_recv()
+        for copy in gather_routes(d):
             copy.wait_recv()
 
     block = min(total, ROW_BLOCK)
@@ -242,11 +254,13 @@
 
         project_down(2 * i + 1, own)
 
-        @pl.when(i > 0)
+        @pl.when(i > 1)
         def _():
-            add_and_send(i - 1)
+            add_and_send(i - 2)
 
     add_mate(grp - 1)
+    if grp > 1:
+        add_and_send(grp - 2)
     result = add_sources(grp - 1)
     for i in range(grp - 1):
         to_group(i).wait_recv()
@@ -257,9 +271,11 @@
 
     @pl.loop(1, ep)
     def _(d):
-        for copy in gather_copies(d):
+        for copy in gather_routes(d):
             copy.wait_send()
-        pass_on(d).wait_send()
+        for p in range(PIECES):
+            gather_piece(d, p).wait_send()
+            pass_on(d, p).wait_send()
 
     @pl.loop(0, grp)
     def _(i):
@@ -304,8 +320,8 @@
             pltpu.VMEM((grp, rows, share), bf16),
             pltpu.VMEM((grp, rows, share), bf16),
             dma((slots, 2)), dma((down_slots,)), dma((1,)),
-            dma((ep,)), dma((ep,)), dma((ep,)), dma((ep,)), dma((ep,)), dma((ep,)),
-            dma((ep,)), dma((ep,)),
+            dma((ep, PIECES)), dma((ep, PIECES)), dma((ep,)), dma((ep,)), dma((ep,)), dma((ep,)),
+            dma((ep, PIECES)), dma((ep, PIECES)),
             dma((grp,)), dma((grp,)), dma((grp, ep)), dma((grp, ep)), dma((grp,)), dma((grp,)),
         ],
         compiler_params=pltpu.CompilerParams(

time: 57.6 us -> 51.8 us (0.90)
  Pallas kernels: 53 us -> 47.2 us
    pallas_call x1, Pallas kernels: 53 us -> 47.2 us  [local(): pl.pallas_call(functools.partial(kernel, ep, grp, tp), out_shape=jax.Shap...]
where the time goes in v2:
time: 51.8 us; the launch traced here: 51.4 us
  Pallas kernels  47.2 us (91%)
  local copies, waits for them, and re-layouts  4.17 us (8%)
    pallas_call x1, Pallas kernels, local(): pl.pallas_call(functools.partial(kernel, ep, grp, tp), out_shape=jax.Shap...  47.2 us
    unnamed x3, local copies, waits for them, and re-layouts  4.17 us

profile of v2, /device:TPU:0, one launch (start us, length us, event | category | flops | bytes accessed | tf_op | source)
XLA Modules:
  0.0 51.4 jit_solution(15213056895911581340)
XLA Ops:
  0.0 1.4 %copy.7.gates = f32[32,8]{1,0:T(8,128)} copy(f32[32,8]{0,1:T(8,128)} %param.7) | data formatting | bytes 2048 | tf_op args[1]
  1.4 1.4 %copy.8.ids = s32[32,8]{1,0:T(8,128)} copy(s32[32,8]{0,1:T(8,128)} %param.8) | data formatting | bytes 2048 | tf_op args[2]
  2.7 47.2 %shard_map.64 = bf16[32,896]{1,0:T(8,128)(2,1)} custom-call(bf16[32,3584]{1,0:T(8,128)(2,1)} %tok.1, f32[32,8]{1,0:T(8,128)} %copy.7.gates, s32[32,8]{1,0:T(8,128)} %copy.8.ids, bf16[8,7168,256]{2,1,0:T(8,128)(2,1)} %wg.1, bf16[8,7168,256]{2,1,0:T(8,128)(2,1)} %wu.1, bf16[2048,7168]{1,0:T(8,128)(2,1)} %bitcast.1), custom_call_target="tpu_custom_call" | custom-call | tf_op jit(solution)/shard_map/pallas_call | solution.py:302
  49.9 1.4 %copy.10 = bf16[32,896]{1,0:T(8,128)(2,1)} copy(bf16[32,896]{1,0:T(8,128)(2,1)} %shard_map.64) | data formatting | bytes 114688
